TPU v7x, 512 devices: a whole 4x8x8 slice. The times are simulated.
512 devices in a mesh: date: 16 (over z, x_hi), trade: 16 (over y, core), path: 2 (over x_lo).
Axes of the slice: x: 4 (x_hi: 2, x_lo: 2; x = x_hi * 2 + x_lo), y: 8, z: 8, core: 2. Of those that a mesh axis runs over, the one named last changes fastest.
Arguments:
- normals: bfloat16 [32, 64, 8192], P('date', None, ('trade', 'path')), may hold values from -6 to 6
- chol: float32 [64, 64], replicated, as said below
- volatility: float32 [64], replicated, may hold values from 0.5 to 2
- start_state: float32 [64], replicated, may hold values from -3 to 3
- basis_map: float32 [64, 128], replicated, may hold values from -0.75 to 0.75
- basis_bias: float32 [128], replicated, may hold values from -3 to 3
- coef: bfloat16 [128, 16384], P(None, 'trade'), may hold values from -0.5 to 0.5
- maturity: int32 [16384], P('trade'), may hold values from 1 to 32
- netting: int32 [16384], P('trade'), may hold values from 0 to 2047, as said below
Outputs:
- exposure: float32 [32, 2048], P('date', 'trade')
Inputs may be any that keep to these rules, and one draw needn't show every extreme that they name: netting sets are whole within a shard of trades: netting[j] // 128 == j // 1024, and every netting set holds at least one trade. `chol`: lower triangular with a positive diagonal.
All inputs are finite; a program needn't handle non-finite values.
Results may differ from a plain program's by a relative error of at most 0.00035.
Values may be sent and summed in bfloat16 or wider, within the bound.
A program may use at most 64 MiB of HBM per device.

v0:
```python
import jax
import jax.numpy as jnp
from jax import lax
from jax.sharding import PartitionSpec as P

NS_DEV = 128


def entering(array, axis, join, neutral):
    place = lax.axis_index(axis)
    gathered = lax.all_gather(array.astype(jnp.bfloat16), axis)
    state = jnp.zeros_like(array) + jnp.asarray(neutral, array.dtype)

    def one(lap, state):
        return join(state, lax.dynamic_index_in_dim(gathered, lap, 0, False).astype(array.dtype))

    return lax.fori_loop(0, place, one, state)


def add_pair(earlier, later):
    return earlier + later


def local_moves(draws, chol, volatility, date_total):
    scale = volatility * jnp.sqrt(jnp.float32(1.0) / date_total)
    moves = jnp.einsum(
        "fg,tgp->tfp", chol, draws.astype(jnp.float32), precision=lax.Precision.HIGHEST
    )
    return jnp.cumsum(moves * scale[None, :, None], axis=0)


def shards(normals, chol, volatility, start_state, basis_map, basis_bias, coef, maturity, netting):
    date_count, factor_count, path_count = normals.shape
    trade_count = coef.shape[1]
    set_count = trade_count * 0 + NS_DEV
    date_total = date_count * lax.axis_size("date")
    path_total = path_count * lax.axis_size("trade") * lax.axis_size("path")
    first_date = lax.axis_index("date") * date_count
    when = first_date + jnp.arange(date_count, dtype=jnp.int32)
    alive = (when[:, None] < maturity[None, :]).astype(jnp.float32)
    local_set = netting - lax.axis_index("trade") * set_count
    member = (local_set[:, None] == jnp.arange(set_count, dtype=jnp.int32)[None, :]).astype(
        jnp.bfloat16
    )
    own_local = local_moves(normals, chol, volatility, date_total)
    empty = jnp.zeros_like(own_local[-1])
    prior = entering(own_local[-1], "date", add_pair, empty)
    states = start_state[None, :, None] + prior[None] + own_local
    pre = jnp.einsum(
        "tfp,fk->tpk",
        lax.all_gather(states, "trade", axis=2, tiled=True),
        basis_map,
        precision=lax.Precision.HIGHEST,
    )
    basis = jnp.tanh(pre + basis_bias[None, None, :]).astype(jnp.bfloat16)
    value = jnp.einsum("tpk,kj->tpj", basis, coef, preferred_element_type=jnp.float32)
    value = (value * alive[:, None, :]).astype(jnp.bfloat16)
    net = jnp.einsum("tpj,js->tps", value, member, preferred_element_type=jnp.float32)
    total = jnp.sum(jnp.maximum(net, 0.0), axis=1)
    summed = lax.psum(total, "path")
    return summed / path_total


def solution(mesh):
    placed = (
        P("date", None, ("trade", "path")),
        P(),
        P(),
        P(),
        P(),
        P(),
        P(None, "trade"),
        P("trade"),
        P("trade"),
    )
    return jax.shard_map(
        shards, mesh=mesh, in_specs=placed, out_specs=P("date", "trade"), check_vma=False
    )
```

profile of v0, /device:TPU:1, one launch (start us, length us, event | category | flops | bytes accessed | tf_op | source)
XLA Modules:
  0.0 125.8 jit_solution(15111759457493451321)
XLA Ops:
  6.5 0.0 copy-start
  6.5 0.0 copy-start.4
  6.5 0.0 copy-start.3
  6.5 0.0 copy-start.2
  6.5 0.0 copy-start.1
  6.5 0.0 copy-start.5
  6.6 0.0 all-gather.2.cloned.1.call-start
  6.6 0.7 broadcast_multiply_fusion.1
  7.3 1.0 fusion.8
  8.4 0.1 fusion.16
  8.5 43.9 %all_gather.7 = bf16[16,64,256]{2,1,0:T(8,128)(2,1)S(1)} all-gather(bf16[1,64,256]{2,1,0:T(8,128)(2,1)S(1)} %slice.7), channel_id=1, replica_groups=mesh['date'=16,'trade'=16,'path'=2] {'date'}, dimensions={0}, use_global_device_ids=true | all-gather | bytes 557056 | tf_op jit(solution)/shard_map/all_gather | solution.py:11
  52.4 0.0 copy-done.4
  52.4 0.1 broadcast_add_fusion.1
  52.5 0.7 broadcast_add_fusion
  53.2 0.0 all-gather.2.cloned.1.call-update
  53.2 0.0 copy-done.3
  53.2 0.0 copy-done.2
  53.2 0.1 compare_convert_fusion
  53.3 43.9 %all-gather.2.cloned.1.call-done = f32[2,64,4096]{2,1,0:T(8,128)} async-done(((f32[2,64,256]{2,1,0:T(8,128)}), f32[2,64,4096]{2,1,0:T(8,128)}) %all-gather.2.cloned.1.call-update) | async-done | bytes 2097168 | tf_op jit(solution)/shard_map/all_gather | solution.py:51
  97.2 0.0 copy-done.1
  97.2 0.0 copy-done.5
  97.2 8.3 %fusion.6 = bf16[2,4096,128]{2,1,0:T(8,128)(2,1)S(1)} fusion(f32[2,64,4096]{2,1,0:T(8,128)} %all-gather.2.cloned.1.call-done, f32[128]{0:T(128)S(1)} %copy-done.5, f32[64,128]{1,0:T(8,128)S(1)} %copy-done.1), kind=kOutput, calls=%fused_computation.8 | convolution fusion | flops 807403520 | bytes 4227584 | tf_op jit(solution)/shard_map/tfp,fk->tpk/dot_general | solution.py:49
  105.5 0.0 copy-done
  105.5 9.0 %fusion.7 = f32[2,128]{1,0:T(2,128)S(1)} fusion(f32[2,1024]{1,0:T(2,128)S(1)} %compare_convert_fusion, bf16[2,4096,128]{2,1,0:T(8,128)(2,1)S(1)} %fusion.6, bf16[128,1024]{1,0:T(8,128)(2,1)S(1)} %copy-done, s32[1024]{0:T(1024)S(1)} %broadcast_subtract_fusion), kind=kOutput, calls=%fused_computation.9 | convolution fusion | flops 4313972736 | bytes 2372608 | tf_op jit(solution)/shard_map/tpj,js->tps/dot_general | solution.py:58
  114.6 3.8 %psum.7 = f32[2,128]{1,0:T(2,128)S(1)} all-reduce(f32[2,128]{1,0:T(2,128)S(1)} %fusion.7), channel_id=1, replica_groups=mesh['date'=16,'trade'=16,'path'=2] {'path'}, use_global_device_ids=true, to_apply=%region_4.5 | all-reduce | flops 256 | bytes 2048 | tf_op jit(solution)/shard_map/psum | solution.py:60
  118.3 0.6 broadcast_multiply_fusion
  (5 shorter events, 0.0 us)
Async XLA Ops:
  6.5 99.0 %copy-start = (bf16[128,1024]{1,0:T(8,128)(2,1)S(1)}, bf16[128,1024]{1,0:T(8,128)(2,1)}, u32[]{:S(2)}) copy-start(bf16[128,1024]{1,0:T(8,128)(2,1)} %param.17) | copy-start | bytes 786436
  6.5 45.9 %copy-start.4 = (f32[64]{0:T(128)S(1)}, f32[64]{0:T(128)}, u32[]{:S(2)}) copy-start(f32[64]{0:T(128)} %param.14) | copy-start | bytes 772
  6.5 46.7 %copy-start.3 = (s32[1024]{0:T(1024)S(1)}, s32[1024]{0:T(1024)}, u32[]{:S(2)}) copy-start(s32[1024]{0:T(1024)} %param.19) | copy-start | bytes 12292
  6.5 46.7 %copy-start.2 = (s32[1024]{0:T(1024)S(1)}, s32[1024]{0:T(1024)}, u32[]{:S(2)}) copy-start(s32[1024]{0:T(1024)} %param.18) | copy-start | bytes 12292
  6.5 90.6 %copy-start.1 = (f32[64,128]{1,0:T(8,128)S(1)}, f32[64,128]{1,0:T(8,128)}, u32[]{:S(2)}) copy-start(f32[64,128]{1,0:T(8,128)} %param.15) | copy-start | bytes 98308
  6.5 90.6 %copy-start.5 = (f32[128]{0:T(128)S(1)}, f32[128]{0:T(128)}, u32[]{:S(2)}) copy-start(f32[128]{0:T(128)} %param.16) | copy-start | bytes 1540
  6.6 90.6 %all-gather.2.cloned.1.call-start = ((), (), s32[]{:S(2)}) async-start(), calls=%async_computation | async-start | bytes 2228224 | tf_op jit(solution)/shard_map/all_gather | solution.py:51
Sparse Core Ops, SparseCore 0:
  53.3 43.8 all-gather.1
where the time goes:
time: 126 us
  blocking collectives  47.7 us (38%)
  waiting for transfers between devices  43.9 us (35%)
  matrix products  18.4 us (15%)
  between operations  13.5 us (11%)
  other arithmetic  2.22 us (2%)
    all_gather x1, blocking collectives, entering(): gathered = lax.all_gather(array.astype(jnp.bfloat16), axis)  43.9 us
    all_gather x1, waiting for transfers between devices, shards(): lax.all_gather(states, 'trade', axis=2, tiled=True)  43.9 us
    dot_general x1, matrix products, shards(): jnp.einsum('tpj,js->tps', value, member, preferred_element_type=jnp.float32)  9.03 us
    dot_general x1, matrix products, shards(): jnp.einsum('tfp,fk->tpk', lax.all_gather(states, 'trade', axis=2, tiled=T...  8.32 us
    psum x1, blocking collectives, shards(): summed = lax.psum(total, 'path')  3.79 us
  transfers between devices with their start and end apart: 1, of which 1 were waited for; matrix products, arithmetic and copies ran while one was open for 0% of the time, Pallas kernels for 0%

commit v1 on v0

--- a/solution.py
+++ b/solution.py
@@ -4,6 +4,24 @@
 from jax.sharding import PartitionSpec as P
 
 NS_DEV = 128
+
+
+def collect(shard, axis, dim):
+    ways, here, hop = (lax.axis_size(axis), lax.axis_index(axis), shard.shape[dim])
+    dims = [n * ways if d == dim else n for d, n in enumerate(shard.shape)]
+    full = lax.dynamic_update_slice_in_dim(
+        jnp.zeros(dims, shard.dtype), shard, here * hop, axis=dim
+    )
+    going_up = going_down = shard
+    for far in range(1, ways // 2 + 1):
+        going_up = lax.ppermute(going_up, axis, [(d, (d + 1) % ways) for d in range(ways)])
+        full = lax.dynamic_update_slice_in_dim(full, going_up, (here - far) % ways * hop, axis=dim)
+        if 2 * far < ways:
+            going_down = lax.ppermute(going_down, axis, [(d, (d - 1) % ways) for d in range(ways)])
+            full = lax.dynamic_update_slice_in_dim(
+                full, going_down, (here + far) % ways * hop, axis=dim
+            )
+    return full
 
 
 def entering(array, axis, join, neutral):
@@ -47,10 +65,7 @@
     prior = entering(own_local[-1], "date", add_pair, empty)
     states = start_state[None, :, None] + prior[None] + own_local
     pre = jnp.einsum(
-        "tfp,fk->tpk",
-        lax.all_gather(states, "trade", axis=2, tiled=True),
-        basis_map,
-        precision=lax.Precision.HIGHEST,
+        "tfp,fk->tpk", collect(states, "trade", 2), basis_map, precision=lax.Precision.HIGHEST
     )
     basis = jnp.tanh(pre + basis_bias[None, None, :]).astype(jnp.bfloat16)
     value = jnp.einsum("tpk,kj->tpj", basis, coef, preferred_element_type=jnp.float32)

time: 126 us -> 121 us (0.960)
  the two profiles are of different devices: /device:TPU:1 before, /device:TPU:32 now
where the time goes in v1:
time: 121 us
  blocking collectives  54.8 us (45%)
  waiting for transfers between devices  23.7 us (20%)
  starting transfers between devices  20.7 us (17%)
  matrix products  19.5 us (16%)
  other arithmetic  1.57 us (1%)
    all_gather x1, blocking collectives, entering(): gathered = lax.all_gather(array.astype(jnp.bfloat16), axis)  49.8 us
    ppermute x8, waiting for transfers between devices, collect(): lax.ppermute(going_up, axis, [(d, (d + 1) % ways) for d in range(ways)])  23.7 us
    ppermute x7, starting transfers between devices, collect(): lax.ppermute(going_down, axis, [(d, (d - 1) % ways) for d in range(ways)])  20.7 us
    dot_general x1, matrix products, shards(): jnp.einsum('tpj,js->tps', value, member, preferred_element_type=jnp.float32)  10.6 us
    dot_general x1, matrix products, shards(): jnp.einsum('tfp,fk->tpk', collect(states, 'trade', 2), basis_map, precisi...  7.9 us
    psum x1, blocking collectives, shards(): summed = lax.psum(total, 'path')  4.94 us
  transfers between devices with their start and end apart: 15, of which 8 were waited for; matrix products, arithmetic and copies ran while one was open for 0% of the time, Pallas kernels for 0%

profile of v1, /device:TPU:32, one launch (start us, length us, event | category | flops | bytes accessed | tf_op | source)
XLA Modules:
  0.0 121.0 jit_solution(15675385401940018500)
XLA Ops:
  0.0 0.7 broadcast_multiply_fusion.1
  0.7 1.0 fusion.8
  1.8 0.1 fusion.16
  1.9 49.8 %all_gather.4 = bf16[16,64,256]{2,1,0:T(8,128)(2,1)S(1)} all-gather(bf16[1,64,256]{2,1,0:T(8,128)(2,1)S(1)} %slice.7), channel_id=1, replica_groups=mesh['date'=16,'trade'=16,'path'=2] {'date'}, dimensions={0}, use_global_device_ids=true | all-gather | bytes 557056 | tf_op jit(solution)/shard_map/all_gather | solution.py:29
  51.7 0.0 copy-start.3
  51.8 0.1 broadcast_add_fusion.1
  51.9 0.2 broadcast_in_dim.4
  52.1 0.0 collective-permute-start
  52.1 2.9 %collective-permute-start.1 = (f32[2,64,256]{2,1,0:T(8,128)S(1)}, f32[2,64,256]{2,1,0:T(8,128)S(1)}, u32[]{:S(2)}, u32[]{:S(2)}) collective-permute-start(f32[2,64,256]{2,1,0:T(8,128)S(1)} %get-tuple-element.38), channel_id=1, source_target_pairs={{0,30},{2,0},{4,2},{6,4},{8,6},{10,8},{12,10},{14,12},{16,14},{18,... | collective-permute-start | bytes 393224 | tf_op jit(solution)/shard_map/ppermute | solution.py:20
  55.1 0.1 compare_convert_fusion
  55.2 2.6 %collective-permute-done = f32[2,64,256]{2,1,0:T(8,128)S(1)} collective-permute-done((f32[2,64,256]{2,1,0:T(8,128)S(1)}, f32[2,64,256]{2,1,0:T(8,128)S(1)}, u32[]{:S(2)}, u32[]{:S(2)}) %collective-permute-start) | collective-permute-done | bytes 131104 | tf_op jit(solution)/shard_map/ppermute | solution.py:17
  57.7 0.0 collective-permute-start.2
  57.7 0.0 collective-permute-done.1
  57.7 3.0 %collective-permute-start.3 = (f32[2,64,256]{2,1,0:T(8,128)S(1)}, f32[2,64,256]{2,1,0:T(8,128)S(1)}, u32[]{:S(2)}, u32[]{:S(2)}) collective-permute-start(f32[2,64,256]{2,1,0:T(8,128)S(1)} %collective-permute-done.1), channel_id=1, source_target_pairs={{0,30},{2,0},{4,2},{6,4},{8,6},{10,8},{12,10},{14,12},{16,14},{18,... | collective-permute-start | bytes 393224 | tf_op jit(solution)/shard_map/ppermute | solution.py:20
  60.7 2.6 %collective-permute-done.2 = f32[2,64,256]{2,1,0:T(8,128)S(1)} collective-permute-done((f32[2,64,256]{2,1,0:T(8,128)S(1)}, f32[2,64,256]{2,1,0:T(8,128)S(1)}, u32[]{:S(2)}, u32[]{:S(2)}) %collective-permute-start.2) | collective-permute-done | bytes 131104 | tf_op jit(solution)/shard_map/ppermute | solution.py:17
  63.3 3.0 %collective-permute-start.5 = (f32[2,64,256]{2,1,0:T(8,128)S(1)}, f32[2,64,256]{2,1,0:T(8,128)S(1)}, u32[]{:S(2)}, u32[]{:S(2)}) collective-permute-start(f32[2,64,256]{2,1,0:T(8,128)S(1)} %collective-permute-done.3), channel_id=1, source_target_pairs={{0,30},{2,0},{4,2},{6,4},{8,6},{10,8},{12,10},{14,12},{16,14},{18,... | collective-permute-start | bytes 393224 | tf_op jit(solution)/shard_map/ppermute | solution.py:20
  66.3 2.6 %collective-permute-done.4 = f32[2,64,256]{2,1,0:T(8,128)S(1)} collective-permute-done((f32[2,64,256]{2,1,0:T(8,128)S(1)}, f32[2,64,256]{2,1,0:T(8,128)S(1)}, u32[]{:S(2)}, u32[]{:S(2)}) %collective-permute-start.4) | collective-permute-done | bytes 131104 | tf_op jit(solution)/shard_map/ppermute | solution.py:17
  68.9 0.0 collective-permute-start.6
  68.9 0.0 collective-permute-done.5
  68.9 3.0 %collective-permute-start.7 = (f32[2,64,256]{2,1,0:T(8,128)S(1)}, f32[2,64,256]{2,1,0:T(8,128)S(1)}, u32[]{:S(2)}, u32[]{:S(2)}) collective-permute-start(f32[2,64,256]{2,1,0:T(8,128)S(1)} %collective-permute-done.5), channel_id=1, source_target_pairs={{0,30},{2,0},{4,2},{6,4},{8,6},{10,8},{12,10},{14,12},{16,14},{18,... | collective-permute-start | bytes 393224 | tf_op jit(solution)/shard_map/ppermute | solution.py:20
  71.9 2.6 %collective-permute-done.6 = f32[2,64,256]{2,1,0:T(8,128)S(1)} collective-permute-done((f32[2,64,256]{2,1,0:T(8,128)S(1)}, f32[2,64,256]{2,1,0:T(8,128)S(1)}, u32[]{:S(2)}, u32[]{:S(2)}) %collective-permute-start.6) | collective-permute-done | bytes 131104 | tf_op jit(solution)/shard_map/ppermute | solution.py:17
  74.5 3.0 %collective-permute-start.9 = (f32[2,64,256]{2,1,0:T(8,128)S(1)}, f32[2,64,256]{2,1,0:T(8,128)S(1)}, u32[]{:S(2)}, u32[]{:S(2)}) collective-permute-start(f32[2,64,256]{2,1,0:T(8,128)S(1)} %collective-permute-done.7), channel_id=1, source_target_pairs={{0,30},{2,0},{4,2},{6,4},{8,6},{10,8},{12,10},{14,12},{16,14},{18,... | collective-permute-start | bytes 393224 | tf_op jit(solution)/shard_map/ppermute | solution.py:20
  77.5 2.6 %collective-permute-done.8 = f32[2,64,256]{2,1,0:T(8,128)S(1)} collective-permute-done((f32[2,64,256]{2,1,0:T(8,128)S(1)}, f32[2,64,256]{2,1,0:T(8,128)S(1)}, u32[]{:S(2)}, u32[]{:S(2)}) %collective-permute-start.8) | collective-permute-done | bytes 131104 | tf_op jit(solution)/shard_map/ppermute | solution.py:17
  80.1 3.0 %collective-permute-start.11 = (f32[2,64,256]{2,1,0:T(8,128)S(1)}, f32[2,64,256]{2,1,0:T(8,128)S(1)}, u32[]{:S(2)}, u32[]{:S(2)}) collective-permute-start(f32[2,64,256]{2,1,0:T(8,128)S(1)} %collective-permute-done.9), channel_id=1, source_target_pairs={{0,30},{2,0},{4,2},{6,4},{8,6},{10,8},{12,10},{14,12},{16,14},{18,... | collective-permute-start | bytes 393224 | tf_op jit(solution)/shard_map/ppermute | solution.py:20
  83.1 2.6 %collective-permute-done.10 = f32[2,64,256]{2,1,0:T(8,128)S(1)} collective-permute-done((f32[2,64,256]{2,1,0:T(8,128)S(1)}, f32[2,64,256]{2,1,0:T(8,128)S(1)}, u32[]{:S(2)}, u32[]{:S(2)}) %collective-permute-start.10) | collective-permute-done | bytes 131104 | tf_op jit(solution)/shard_map/ppermute | solution.py:17
  85.7 3.0 %collective-permute-start.13 = (f32[2,64,256]{2,1,0:T(8,128)S(1)}, f32[2,64,256]{2,1,0:T(8,128)S(1)}, u32[]{:S(2)}, u32[]{:S(2)}) collective-permute-start(f32[2,64,256]{2,1,0:T(8,128)S(1)} %collective-permute-done.11), channel_id=1, source_target_pairs={{0,30},{2,0},{4,2},{6,4},{8,6},{10,8},{12,10},{14,12},{16,14},{18,... | collective-permute-start | bytes 393224 | tf_op jit(solution)/shard_map/ppermute | solution.py:20
  88.7 2.6 %collective-permute-done.12 = f32[2,64,256]{2,1,0:T(8,128)S(1)} collective-permute-done((f32[2,64,256]{2,1,0:T(8,128)S(1)}, f32[2,64,256]{2,1,0:T(8,128)S(1)}, u32[]{:S(2)}, u32[]{:S(2)}) %collective-permute-start.12) | collective-permute-done | bytes 131104 | tf_op jit(solution)/shard_map/ppermute | solution.py:17
  91.4 5.5 %collective-permute-done.14 = f32[2,64,256]{2,1,0:T(8,128)S(1)} collective-permute-done((f32[2,64,256]{2,1,0:T(8,128)S(1)}, f32[2,64,256]{2,1,0:T(8,128)S(1)}, u32[]{:S(2)}, u32[]{:S(2)}) %collective-permute-start.14) | collective-permute-done | bytes 131104 | tf_op jit(solution)/shard_map/ppermute | solution.py:17
  97.0 7.9 %fusion.6 = bf16[2,4096,128]{2,1,0:T(8,128)(2,1)} fusion(f32[2,64,4096]{2,1,0:T(8,128)S(1)} %constant_dynamic-update-slice_fusion, f32[128]{0:T(128)S(1)} %copy-done.5, f32[64,128]{1,0:T(8,128)S(1)} %copy-done.1), kind=kOutput, calls=%fused_computation.8 | convolution fusion | flops 807403520 | bytes 4227584 | tf_op jit(solution)/shard_map/tfp,fk->tpk/dot_general | solution.py:67
  104.9 10.6 %fusion.7 = f32[2,128]{1,0:T(2,128)S(1)} fusion(f32[2,1024]{1,0:T(2,128)S(1)} %compare_convert_fusion, bf16[2,4096,128]{2,1,0:T(8,128)(2,1)} %fusion.6, bf16[128,1024]{1,0:T(8,128)(2,1)S(1)} %copy-done, s32[1024]{0:T(1024)S(1)} %broadcast_subtract_fusion), kind=kOutput, calls=%fused_computation.9 | convolution fusion | flops 4313972736 | bytes 2372608 | tf_op jit(solution)/shard_map/tpj,js->tps/dot_general | solution.py:73
  115.5 4.9 %psum.7 = f32[2,128]{1,0:T(2,128)S(1)} all-reduce(f32[2,128]{1,0:T(2,128)S(1)} %fusion.7), channel_id=1, replica_groups=mesh['date'=16,'trade'=16,'path'=2] {'path'}, use_global_device_ids=true, to_apply=%region_4.5 | all-reduce | flops 256 | bytes 2048 | tf_op jit(solution)/shard_map/psum | solution.py:75
  120.4 0.6 broadcast_multiply_fusion
  (42 shorter events, 0.3 us)
Async XLA Ops:
  0.0 104.9 %copy-start = (bf16[128,1024]{1,0:T(8,128)(2,1)S(1)}, bf16[128,1024]{1,0:T(8,128)(2,1)}, u32[]{:S(2)}) copy-start(bf16[128,1024]{1,0:T(8,128)(2,1)} %param.17) | copy-start | bytes 786436
  0.0 51.8 %copy-start.4 = (f32[64]{0:T(128)S(1)}, f32[64]{0:T(128)}, u32[]{:S(2)}) copy-start(f32[64]{0:T(128)} %param.14) | copy-start | bytes 772
  51.7 3.3 %copy-start.2 = (s32[1024]{0:T(1024)S(1)}, s32[1024]{0:T(1024)}, u32[]{:S(2)}) copy-start(s32[1024]{0:T(1024)} %param.18) | copy-start | bytes 12292
  51.7 3.4 %copy-start.3 = (s32[1024]{0:T(1024)S(1)}, s32[1024]{0:T(1024)}, u32[]{:S(2)}) copy-start(s32[1024]{0:T(1024)} %param.19) | copy-start | bytes 12292
  52.1 5.6 %collective-permute-start = (f32[2,64,256]{2,1,0:T(8,128)S(1)}, f32[2,64,256]{2,1,0:T(8,128)S(1)}, u32[]{:S(2)}, u32[]{:S(2)}) collective-permute-start(f32[2,64,256]{2,1,0:T(8,128)S(1)} %get-tuple-element.38), channel_id=1, source_target_pairs={{0,2},{2,4},{4,6},{6,8},{8,10},{10,12},{12,14},{14,16},{16,18},{18... | collective-permute-start | bytes 393224 | tf_op jit(solution)/shard_map/ppermute | solution.py:17
  52.1 5.6 %collective-permute-start.1 = (f32[2,64,256]{2,1,0:T(8,128)S(1)}, f32[2,64,256]{2,1,0:T(8,128)S(1)}, u32[]{:S(2)}, u32[]{:S(2)}) collective-permute-start(f32[2,64,256]{2,1,0:T(8,128)S(1)} %get-tuple-element.38), channel_id=1, source_target_pairs={{0,30},{2,0},{4,2},{6,4},{8,6},{10,8},{12,10},{14,12},{16,14},{18,... | collective-permute-start | bytes 393224 | tf_op jit(solution)/shard_map/ppermute | solution.py:20
  55.1 41.9 %copy-start.1 = (f32[64,128]{1,0:T(8,128)S(1)}, f32[64,128]{1,0:T(8,128)}, u32[]{:S(2)}) copy-start(f32[64,128]{1,0:T(8,128)} %param.15) | copy-start | bytes 98308
  55.1 41.9 %copy-start.5 = (f32[128]{0:T(128)S(1)}, f32[128]{0:T(128)}, u32[]{:S(2)}) copy-start(f32[128]{0:T(128)} %param.16) | copy-start | bytes 1540
  57.7 5.6 %collective-permute-start.2 = (f32[2,64,256]{2,1,0:T(8,128)S(1)}, f32[2,64,256]{2,1,0:T(8,128)S(1)}, u32[]{:S(2)}, u32[]{:S(2)}) collective-permute-start(f32[2,64,256]{2,1,0:T(8,128)S(1)} %collective-permute-done), channel_id=1, source_target_pairs={{0,2},{2,4},{4,6},{6,8},{8,10},{10,12},{12,14},{14,16},{16,18},{18... | collective-permute-start | bytes 393224 | tf_op jit(solution)/shard_map/ppermute | solution.py:17
  57.7 5.6 %collective-permute-start.3 = (f32[2,64,256]{2,1,0:T(8,128)S(1)}, f32[2,64,256]{2,1,0:T(8,128)S(1)}, u32[]{:S(2)}, u32[]{:S(2)}) collective-permute-start(f32[2,64,256]{2,1,0:T(8,128)S(1)} %collective-permute-done.1), channel_id=1, source_target_pairs={{0,30},{2,0},{4,2},{6,4},{8,6},{10,8},{12,10},{14,12},{16,14},{18,... | collective-permute-start | bytes 393224 | tf_op jit(solution)/shard_map/ppermute | solution.py:20
  63.3 5.6 %collective-permute-start.4 = (f32[2,64,256]{2,1,0:T(8,128)S(1)}, f32[2,64,256]{2,1,0:T(8,128)S(1)}, u32[]{:S(2)}, u32[]{:S(2)}) collective-permute-start(f32[2,64,256]{2,1,0:T(8,128)S(1)} %collective-permute-done.2), channel_id=1, source_target_pairs={{0,2},{2,4},{4,6},{6,8},{8,10},{10,12},{12,14},{14,16},{16,18},{18... | collective-permute-start | bytes 393224 | tf_op jit(solution)/shard_map/ppermute | solution.py:17
  63.3 5.6 %collective-permute-start.5 = (f32[2,64,256]{2,1,0:T(8,128)S(1)}, f32[2,64,256]{2,1,0:T(8,128)S(1)}, u32[]{:S(2)}, u32[]{:S(2)}) collective-permute-start(f32[2,64,256]{2,1,0:T(8,128)S(1)} %collective-permute-done.3), channel_id=1, source_target_pairs={{0,30},{2,0},{4,2},{6,4},{8,6},{10,8},{12,10},{14,12},{16,14},{18,... | collective-permute-start | bytes 393224 | tf_op jit(solution)/shard_map/ppermute | solution.py:20
  68.9 5.6 %collective-permute-start.6 = (f32[2,64,256]{2,1,0:T(8,128)S(1)}, f32[2,64,256]{2,1,0:T(8,128)S(1)}, u32[]{:S(2)}, u32[]{:S(2)}) collective-permute-start(f32[2,64,256]{2,1,0:T(8,128)S(1)} %collective-permute-done.4), channel_id=1, source_target_pairs={{0,2},{2,4},{4,6},{6,8},{8,10},{10,12},{12,14},{14,16},{16,18},{18... | collective-permute-start | bytes 393224 | tf_op jit(solution)/shard_map/ppermute | solution.py:17
  68.9 5.6 %collective-permute-start.7 = (f32[2,64,256]{2,1,0:T(8,128)S(1)}, f32[2,64,256]{2,1,0:T(8,128)S(1)}, u32[]{:S(2)}, u32[]{:S(2)}) collective-permute-start(f32[2,64,256]{2,1,0:T(8,128)S(1)} %collective-permute-done.5), channel_id=1, source_target_pairs={{0,30},{2,0},{4,2},{6,4},{8,6},{10,8},{12,10},{14,12},{16,14},{18,... | collective-permute-start | bytes 393224 | tf_op jit(solution)/shard_map/ppermute | solution.py:20
  74.5 5.6 %collective-permute-start.8 = (f32[2,64,256]{2,1,0:T(8,128)S(1)}, f32[2,64,256]{2,1,0:T(8,128)S(1)}, u32[]{:S(2)}, u32[]{:S(2)}) collective-permute-start(f32[2,64,256]{2,1,0:T(8,128)S(1)} %collective-permute-done.6), channel_id=1, source_target_pairs={{0,2},{2,4},{4,6},{6,8},{8,10},{10,12},{12,14},{14,16},{16,18},{18... | collective-permute-start | bytes 393224 | tf_op jit(solution)/shard_map/ppermute | solution.py:17
  74.5 5.6 %collective-permute-start.9 = (f32[2,64,256]{2,1,0:T(8,128)S(1)}, f32[2,64,256]{2,1,0:T(8,128)S(1)}, u32[]{:S(2)}, u32[]{:S(2)}) collective-permute-start(f32[2,64,256]{2,1,0:T(8,128)S(1)} %collective-permute-done.7), channel_id=1, source_target_pairs={{0,30},{2,0},{4,2},{6,4},{8,6},{10,8},{12,10},{14,12},{16,14},{18,... | collective-permute-start | bytes 393224 | tf_op jit(solution)/shard_map/ppermute | solution.py:20
  80.1 5.6 %collective-permute-start.10 = (f32[2,64,256]{2,1,0:T(8,128)S(1)}, f32[2,64,256]{2,1,0:T(8,128)S(1)}, u32[]{:S(2)}, u32[]{:S(2)}) collective-permute-start(f32[2,64,256]{2,1,0:T(8,128)S(1)} %collective-permute-done.8), channel_id=1, source_target_pairs={{0,2},{2,4},{4,6},{6,8},{8,10},{10,12},{12,14},{14,16},{16,18},{18... | collective-permute-start | bytes 393224 | tf_op jit(solution)/shard_map/ppermute | solution.py:17
  80.1 5.6 %collective-permute-start.11 = (f32[2,64,256]{2,1,0:T(8,128)S(1)}, f32[2,64,256]{2,1,0:T(8,128)S(1)}, u32[]{:S(2)}, u32[]{:S(2)}) collective-permute-start(f32[2,64,256]{2,1,0:T(8,128)S(1)} %collective-permute-done.9), channel_id=1, source_target_pairs={{0,30},{2,0},{4,2},{6,4},{8,6},{10,8},{12,10},{14,12},{16,14},{18,... | collective-permute-start | bytes 393224 | tf_op jit(solution)/shard_map/ppermute | solution.py:20
  85.7 5.6 %collective-permute-start.12 = (f32[2,64,256]{2,1,0:T(8,128)S(1)}, f32[2,64,256]{2,1,0:T(8,128)S(1)}, u32[]{:S(2)}, u32[]{:S(2)}) collective-permute-start(f32[2,64,256]{2,1,0:T(8,128)S(1)} %collective-permute-done.10), channel_id=1, source_target_pairs={{0,2},{2,4},{4,6},{6,8},{8,10},{10,12},{12,14},{14,16},{16,18},{18... | collective-permute-start | bytes 393224 | tf_op jit(solution)/shard_map/ppermute | solution.py:17
  85.7 5.6 %collective-permute-start.13 = (f32[2,64,256]{2,1,0:T(8,128)S(1)}, f32[2,64,256]{2,1,0:T(8,128)S(1)}, u32[]{:S(2)}, u32[]{:S(2)}) collective-permute-start(f32[2,64,256]{2,1,0:T(8,128)S(1)} %collective-permute-done.11), channel_id=1, source_target_pairs={{0,30},{2,0},{4,2},{6,4},{8,6},{10,8},{12,10},{14,12},{16,14},{18,... | collective-permute-start | bytes 393224 | tf_op jit(solution)/shard_map/ppermute | solution.py:20
  91.3 5.6 %collective-permute-start.14 = (f32[2,64,256]{2,1,0:T(8,128)S(1)}, f32[2,64,256]{2,1,0:T(8,128)S(1)}, u32[]{:S(2)}, u32[]{:S(2)}) collective-permute-start(f32[2,64,256]{2,1,0:T(8,128)S(1)} %collective-permute-done.12), channel_id=1, source_target_pairs={{0,2},{2,4},{4,6},{6,8},{8,10},{10,12},{12,14},{14,16},{16,18},{18... | collective-permute-start | bytes 393224 | tf_op jit(solution)/shard_map/ppermute | solution.py:17
